TPU v7x, 128 devices: a whole 4x4x4 slice. The times are simulated.
128 devices in a mesh: ctx: 32 (over y, z, core), exp: 4 (over x).
Axes of the slice: x: 4, y: 4, z: 4, core: 2. Of those that a mesh axis runs over, the one named last changes fastest.
Arguments:
- inputs: bfloat16 [4096, 4096], P('ctx', 'exp'), may hold values from -6 to 6
- gate_input: bfloat16 [4096, 4096], P('ctx', 'exp')
- b_proj: bfloat16 [4096, 128], P('ctx'), may hold values from -0.5 to 0.5
- c_proj: bfloat16 [4096, 128], P('ctx'), may hold values from -6 to 6
- step_size: float32 [64, 4096], P('exp', 'ctx'), may hold values from 0.03 to 0.3
- decay_rate: float32 [64, 4096], P('exp', 'ctx'), as said below
- skip_gain: float32 [64], P('exp'), may hold values from 0.5 to 2
- start_state: float32 [64, 64, 128], P('exp'), may hold values from -3 to 3
- norm_gain: float32 [4096], P('exp'), may hold values from 0.5 to 1.5
- out_proj: bfloat16 [4096, 4096], P('exp', 'ctx'), may hold values from -0.09375 to 0.09375
- residual: bfloat16 [4096, 4096], P('ctx'), may hold values from -6 to 6
- moe_gain: float32 [4096], replicated, may hold values from 0.5 to 1.5
- w_gate: bfloat16 [32, 4096, 3584], P('ctx', None, 'exp'), may hold values from -0.09375 to 0.09375
- w_up: bfloat16 [32, 4096, 3584], P('ctx', None, 'exp'), may hold values from -0.09375 to 0.09375
- w_down: bfloat16 [32, 3584, 4096], P('ctx', 'exp'), may hold values from -0.0625 to 0.0625
- route_ids: int32 [4096, 2], P('ctx'), may hold values from 0 to 15, all different within a row; in each aligned block of 32 rows (0 to 31, 32 to 63, ...) at most 8 rows name the same one
- route_gates: float32 [4096, 2], P('ctx'), may hold values from 0.3 to 1
Outputs:
- output: bfloat16 [4096, 4096], P(('ctx', 'exp'))
Inputs may be any that keep to these rules, and one draw needn't show every extreme that they name: `route_ids`: each row names two different experts. In each aligned block of 32 rows no expert is named more than 8 times, a bound that some block reaches. `decay_rate`: Non-negative.
All inputs are finite; a program needn't handle non-finite values.
Results may differ from a plain program's by a relative error of at most 0.02.
Values may be sent and summed in bfloat16 or wider, within the bound.
A program may use at most 128 MiB of HBM per device.

v0:
```python
import jax
import jax.numpy as jnp
from jax import lax
from jax.sharding import PartitionSpec as P

PAIR = 2
eps_norm = 1e-05
top_precision = lax.Precision.HIGHEST


def entering(x, axis, join, neutral):
    place = lax.axis_index(axis)
    decay, state = x
    packed = jnp.concatenate(
        [state, jnp.broadcast_to(decay[:, None, None], (state.shape[0], 1, state.shape[2]))], axis=1
    )
    gathered = lax.all_gather(packed.astype(jnp.bfloat16), axis)
    start = jax.tree.map(lambda a, e: jnp.zeros_like(a) + jnp.asarray(e, a.dtype), x, neutral)

    def one(hop, carry):
        block = lax.dynamic_index_in_dim(gathered, hop, 0, False).astype(jnp.float32)
        return join(carry, (block[:, -1, 0], block[:, :-1, :]))

    return lax.fori_loop(0, place, one, start)


def later_state(earlier, later):
    first_decay, first_state = earlier
    second_decay, second_state = later
    return (first_decay * second_decay, second_decay[:, None, None] * first_state + second_state)


def route_ranks(quarter_ids, experts):
    flattened = quarter_ids.reshape(-1)
    onehot = (flattened[:, None] == jnp.arange(experts, dtype=jnp.int32)[None, :]).astype(jnp.int32)
    running = jnp.cumsum(onehot, axis=0)
    rank_ids = jnp.sum(onehot * running, axis=1) - 1
    return (flattened, rank_ids)


def place_rows(normed, quarter_ids, experts, capacity):
    flattened, rank_ids = route_ranks(quarter_ids, experts)
    slot_ids = rank_ids * experts + flattened
    matches = (
        jnp.arange(capacity * experts, dtype=jnp.int32)[:, None] == slot_ids[None, :]
    ).astype(jnp.bfloat16)
    doubled = jnp.repeat(normed, quarter_ids.shape[1], axis=0)
    placed = jnp.dot(matches, doubled, preferred_element_type=jnp.float32).astype(jnp.bfloat16)
    return placed.reshape(capacity, experts, normed.shape[1])


def rms_rows(values, gain_vec):
    scaling = lax.rsqrt(jnp.mean(values * values, axis=1, keepdims=True) + eps_norm)
    return (values * scaling * gain_vec[None, :]).astype(jnp.bfloat16)


def local(
    inputs,
    gate_input,
    b_proj,
    c_proj,
    step_size,
    decay_rate,
    skip_gain,
    start_state,
    norm_gain,
    out_proj,
    residual,
    moe_gain,
    w_gate,
    w_up,
    w_down,
    route_ids,
    route_gates,
):
    tok_ctx = inputs.shape[0]
    head_count = step_size.shape[0]
    head_dim = inputs.shape[1] // head_count
    model_width = residual.shape[1]
    n_ctx = lax.axis_size("ctx")
    n_exp = lax.axis_size("exp")
    experts = n_ctx // PAIR
    tok_quarter = tok_ctx // n_exp
    capacity = 4 * tok_quarter // experts
    x_local = inputs.astype(jnp.float32).reshape(tok_ctx, head_count, head_dim)
    b_local = b_proj.astype(jnp.float32)
    c_local = c_proj.astype(jnp.float32)
    cumulative = jnp.cumsum(decay_rate, axis=1)
    span_total = cumulative[:, -1]
    sequence_indices = jnp.arange(tok_ctx, dtype=jnp.int32)
    causal = sequence_indices[:, None] >= sequence_indices[None, :]
    spread = jnp.where(causal[None], cumulative[:, :, None] - cumulative[:, None, :], 0.0)
    scores = jnp.dot(c_local, b_local.T, precision=top_precision)
    mixing = jnp.where(causal[None], jnp.exp(-spread), 0.0) * scores[None] * step_size[:, None, :]
    inside_part = jnp.einsum("hts,shp->thp", mixing, x_local, precision=top_precision)
    ending = jnp.exp(-(span_total[:, None] - cumulative)) * step_size
    local_state = jnp.einsum("hs,shp,sn->hpn", ending, x_local, b_local, precision=top_precision)
    prior_decay, prior_state = entering(
        (jnp.exp(-span_total), local_state),
        "ctx",
        later_state,
        (jnp.ones_like(span_total), jnp.zeros_like(local_state)),
    )
    incoming = prior_state + prior_decay[:, None, None] * start_state
    carried = (
        jnp.einsum("hpn,tn->thp", incoming, c_local, precision=top_precision)
        * jnp.exp(-cumulative).T[:, :, None]
    )
    ssm_out = inside_part + carried + skip_gain[None, :, None] * x_local
    gated_out = ssm_out.reshape(tok_ctx, head_count * head_dim) * jax.nn.silu(
        gate_input.astype(jnp.float32)
    )
    squares = lax.psum(jnp.sum(gated_out * gated_out, axis=1), "exp")
    scaling = lax.rsqrt(squares / (head_count * head_dim * n_exp) + eps_norm)
    normed_mix = (gated_out * scaling[:, None] * norm_gain[None, :]).astype(jnp.bfloat16)
    partial_value = jnp.dot(
        normed_mix,
        lax.all_gather(out_proj, "ctx", axis=1, tiled=True),
        preferred_element_type=jnp.float32,
    )
    gate_rows = w_gate[0]
    up_rows = w_up[0]
    down_rows = w_down[0]
    piece_width = gate_rows.shape[1]
    first_row = lax.axis_index("exp") * tok_quarter
    own_ids = lax.dynamic_slice_in_dim(route_ids, first_row, tok_quarter, 0)
    own_gates = lax.dynamic_slice_in_dim(route_gates, first_row, tok_quarter, 0)
    mixed_all = lax.psum(partial_value.astype(jnp.bfloat16), "exp").astype(jnp.float32)
    hidden_all = residual.astype(jnp.float32) + mixed_all
    moe_all = rms_rows(hidden_all, moe_gain)

    def place_quarter(quarter_rows, quarter_ids):
        return place_rows(quarter_rows, quarter_ids, experts, capacity)

    placed = jax.vmap(place_quarter)(
        moe_all.reshape(n_exp, tok_quarter, model_width),
        route_ids.reshape(n_exp, tok_quarter, route_ids.shape[1]),
    )
    placed = placed.reshape(n_exp * capacity, experts, model_width)
    outgoing = jnp.repeat(placed, PAIR, axis=1)
    arrived = lax.all_to_all(outgoing, "ctx", split_axis=1, concat_axis=1, tiled=True)
    flattened = arrived.reshape(-1, model_width)
    gate_val = jnp.dot(flattened, gate_rows, preferred_element_type=jnp.float32)
    up_val = jnp.dot(flattened, up_rows, preferred_element_type=jnp.float32)
    activated = (jax.nn.silu(gate_val) * up_val).astype(jnp.bfloat16)
    hidden = activated.reshape(arrived.shape[0], arrived.shape[1], piece_width)
    hidden_own = lax.dynamic_slice_in_dim(hidden_all, first_row, tok_quarter, 0)
    product = jnp.dot(
        hidden.reshape(-1, piece_width), down_rows, preferred_element_type=jnp.float32
    )
    rounded = lax.optimization_barrier(product.astype(jnp.bfloat16)).astype(jnp.float32)
    summed = lax.psum_scatter(
        rounded.reshape(lax.axis_size("exp") * capacity, hidden.shape[1], model_width).astype(
            jnp.bfloat16
        ),
        "exp",
        scatter_dimension=0,
        tiled=True,
    )
    halves = lax.all_to_all(summed, "ctx", split_axis=1, concat_axis=1, tiled=True)
    flattened, rank_ids = route_ranks(own_ids, experts)
    base_rows = rank_ids * n_ctx + flattened * PAIR
    fetch_rows = base_rows[:, None] + jnp.arange(PAIR, dtype=jnp.int32)[None, :]
    fetched = halves.reshape(capacity * n_ctx, model_width)[fetch_rows]
    expert_out = jnp.sum(fetched.astype(jnp.float32), axis=1)
    weighted = expert_out * own_gates.reshape(-1)[:, None]
    moe_out = jnp.sum(weighted.reshape(tok_quarter, -1, model_width), axis=1)
    return (hidden_own + moe_out).astype(jnp.bfloat16)


def solution(mesh):
    in_specs = (
        P("ctx", "exp"),
        P("ctx", "exp"),
        P("ctx", None),
        P("ctx", None),
        P("exp", "ctx"),
        P("exp", "ctx"),
        P("exp"),
        P("exp", None, None),
        P("exp"),
        P("exp", "ctx"),
        P("ctx", None),
        P(),
        P("ctx", None, "exp"),
        P("ctx", None, "exp"),
        P("ctx", "exp", None),
        P("ctx", None),
        P("ctx", None),
    )
    out_specs = P(("ctx", "exp"), None)
    return jax.shard_map(local, mesh=mesh, in_specs=in_specs, out_specs=out_specs, check_vma=False)
```

profile of v0, /device:TPU:1, one launch (start us, length us, event | category | flops | bytes accessed | tf_op | source)
XLA Modules:
  0.0 688.3 jit_solution(15999288479080339872)
XLA Ops:
  12.6 55.4 %all-gather.3.cloned.1.call-done = bf16[32,16,65,128]{3,1,2,0:T(8,128)(2,1)} async-done(((bf16[1,16,65,128]{3,1,2,0:T(8,128)(2,1)}), bf16[32,16,65,128]{3,1,2,0:T(8,128)(2,1)}) %all-gather.3.cloned.1.call-update) | async-done | bytes 8519696 | tf_op jit(solution)/shard_map/all_gather | solution.py:17
  68.1 2.4 broadcast_in_dim.28
  70.5 7.9 %while.12 = (s32[]{:T(128)}, f32[16]{0:T(128)S(1)}, f32[16,64,128]{0,2,1:T(8,128)}, s32[]{:T(128)}, bf16[32,16,65,128]{3,1,2,0:T(8,128)(2,1)}, /*index=5*/s32[]{:T(128)}, s32[]{:T(128)}, s32[]{:T(128)}) while((s32[]{:T(128)}, f32[16]{0:T(128)S(1)}, f32[16,64,128]{0,2,1:T(8,128)}, s32[]{:T(128)}, bf16[32,16,65,128]{3,1,2,0:T(8,128)(2,1)}, ...), condition=%wide.region_2.3_spmd, body=%wide.region_1.2_spmd.sunk | while | flops 395285 | bytes 3437051 | solution.py:24
  71.5 1.4 copy.132
  73.4 5.0 slice_add_fusion.2
  78.5 3.1 copy.112
  82.1 1.4 fusion.9
  83.9 8.4 %psum.14 = f32[128]{0:T(128)S(1)} all-reduce(f32[128]{0:T(128)S(1)} %multiply_reduce_fusion.2), channel_id=1, replica_groups=mesh['ctx'=32,'exp'=4] {'exp'}, use_global_device_ids=true, to_apply=%region_4.5 | all-reduce | flops 128 | bytes 1024 | tf_op jit(solution)/shard_map/psum | solution.py:113
  92.3 37.1 %all-gather.5.cloned.1.call-done = bf16[1024,4096]{1,0:T(8,128)(2,1)} async-done(((bf16[1024,128]{1,0:T(8,128)(2,1)}), bf16[1024,4096]{1,0:T(8,128)(2,1)}) %all-gather.5.cloned.1.call-update) | async-done | bytes 8388624 | tf_op jit(solution)/shard_map/all_gather | solution.py:118
  129.5 5.8 convolution_convert_fusion.2
  136.3 240.4 %all-reduce.2.cloned.1.call-done = bf16[128,4096]{1,0:T(8,128)(2,1)} async-done(((bf16[128,4096]{1,0:T(8,128)(2,1)}), bf16[128,4096]{1,0:T(8,128)(2,1)}) %all-reduce.2.cloned.1.call-update) | async-done | bytes 1048592 | tf_op jit(solution)/shard_map/psum | solution.py:128
  376.8 3.0 convert_add_fusion
  380.2 3.4 broadcast_in_dim.30
  383.6 2.7 reshape.163
  386.4 1.4 convolution_convert_fusion.1
  387.8 2.3 copy.117
  390.1 4.3 broadcast_in_dim.31
  394.3 105.3 %all_to_all.10 = bf16[32,32,4096]{2,0,1:T(8,128)(2,1)} all-to-all(bf16[32,32,4096]{2,0,1:T(8,128)(2,1)} %bitcast.70), channel_id=1, replica_groups=mesh['ctx'=32,'exp'=4] {'ctx'}, dimensions={1} | all-to-all | bytes 16777216 | tf_op jit(solution)/shard_map/all_to_all | solution.py:141
  499.6 11.3 %copy.118 = bf16[32,32,4096]{2,1,0:T(8,128)(2,1)} copy(bf16[32,32,4096]{2,0,1:T(8,128)(2,1)} %all_to_all.10) | data formatting | bytes 16777216 | tf_op jit(solution)/shard_map/all_to_all | solution.py:141
  511.0 12.7 %fusion.2 = f32[1024,896]{1,0:T(8,128)S(1)} fusion(bf16[1024,4096]{1,0:T(8,128)(2,1)} %bitcast.72, bf16[1,4096,896]{2,1,0:T(8,128)(2,1)} %param.32), kind=kOutput, calls=%fused_computation.8 | convolution fusion | flops 7516192768 | bytes 19398656 | tf_op jit(solution)/shard_map/dot_general | solution.py:144
  523.7 9.2 %multiply_convert_fusion = bf16[1024,896]{1,0:T(8,128)(2,1)S(1)} fusion(f32[1024,896]{1,0:T(8,128)S(1)} %fusion.2, bf16[1024,4096]{1,0:T(8,128)(2,1)S(1)} %bitcast.73, bf16[1,4096,896]{2,1,0:T(8,128)(2,1)S(1)} %bitcast.81), kind=kOutput, calls=%fused_computation.14 | convolution fusion | flops 7521697792 | bytes 21233664 | tf_op jit(solution)/shard_map/dot_general | solution.py:143
  532.9 11.3 %convolution_convert_fusion = bf16[1024,4096]{1,0:T(8,128)(2,1)} fusion(bf16[1024,896]{1,0:T(8,128)(2,1)S(1)} %multiply_convert_fusion, bf16[1,896,4096]{2,1,0:T(8,128)(2,1)S(1)} %bitcast.83), kind=kOutput, calls=%fused_computation.6 | convolution fusion | flops 7520387072 | bytes 17563648 | tf_op jit(solution)/shard_map/dot_general | solution.py:148
  544.1 11.3 %copy.130 = bf16[4,8,32,4096]{3,1,2,0:T(8,128)(2,1)} copy(bf16[4,8,32,4096]{3,2,1,0:T(8,128)(2,1)} %bitcast.74) | data formatting | bytes 16777216
  555.5 77.8 %reduce-scatter.4.cloned.1.call-done = bf16[8,131072]{1,0:T(8,128)(2,1)} async-done(((bf16[32,131072]{1,0:T(8,128)(2,1)}), bf16[8,131072]{1,0:T(8,128)(2,1)}) %reduce-scatter.4.cloned.1.call-update) | async-done | bytes 2097168
  633.2 8.1 %all-to-all-start.1 = ((bf16[8,32,4096]{2,0,1:T(8,128)(2,1)}), bf16[8,32,4096]{2,0,1:T(8,128)(2,1)}, u32[]{:S(2)}, u32[]{:S(2)}) async-start(bf16[8,32,4096]{2,0,1:T(8,128)(2,1)} %bitcast.76), calls=%async_computation.1 | async-start | bytes 4194304 | tf_op jit(solution)/shard_map/all_to_all | solution.py:160
  642.4 27.1 %all-to-all-done.1 = bf16[8,32,4096]{2,0,1:T(8,128)(2,1)} async-done(((bf16[8,32,4096]{2,0,1:T(8,128)(2,1)}), bf16[8,32,4096]{2,0,1:T(8,128)(2,1)}, u32[]{:S(2)}, u32[]{:S(2)}) %all-to-all-start.1) | async-done | bytes 2097184 | tf_op jit(solution)/shard_map/all_to_all | solution.py:160
  669.5 2.7 copy.120
  672.3 1.2 gather_fusion
  673.5 1.3 reshape.178
  674.8 2.7 reduce_sum.60
  678.2 1.4 multiply_reduce_fusion.1
  679.6 1.8 add_convert_fusion
  (87 shorter events, 11.6 us)
Async XLA Ops:
  6.5 3.1 copy-start
  6.5 61.5 %all-gather.3.cloned.1.call-start = ((), (), s32[]{:S(2)}) async-start(), calls=%async_computation.3 | async-start | bytes 8785920 | tf_op jit(solution)/shard_map/all_gather | solution.py:17
  10.9 118.5 %all-gather.5.cloned.1.call-start = ((), (), s32[]{:S(2)}) async-start(), calls=%async_computation.4 | async-start | bytes 8650752 | tf_op jit(solution)/shard_map/all_gather | solution.py:118
  11.7 365.1 %all-reduce.2.cloned.1.call-start = ((), (), s32[]{:S(2)}) async-start(), calls=%async_computation.5 | async-start | bytes 2097152 | tf_op jit(solution)/shard_map/psum | solution.py:128
  78.4 3.1 copy-start.5
  78.4 3.1 copy-start.7
  78.4 3.6 copy-start.9
  78.4 3.6 copy-start.13
  78.5 5.2 copy-start.6
  81.5 47.9 %copy-start.12 = (f32[1024]{0:T(1024)S(1)}, f32[1024]{0:T(1024)}, u32[]{:S(2)}) copy-start(f32[1024]{0:T(1024)} %param.27) | copy-start | bytes 12292
  92.3 43.3 %copy-start.10 = (s32[128,2]{0,1:T(2,128)S(1)}, s32[128,2]{0,1:T(2,128)}, u32[]{:S(2)}) copy-start(s32[128,2]{0,1:T(2,128)} %param.34) | copy-start | bytes 3076
  92.3 284.4 %copy-start.3 = (bf16[128,4096]{1,0:T(8,128)(2,1)S(1)}, bf16[128,4096]{1,0:T(8,128)(2,1)}, u32[]{:S(2)}) copy-start(bf16[128,4096]{1,0:T(8,128)(2,1)} %param.29) | copy-start | bytes 3145732
  135.3 244.5 %copy-start.8 = (f32[4096]{0:T(1024)S(1)}, f32[4096]{0:T(1024)}, u32[]{:S(2)}) copy-start(f32[4096]{0:T(1024)} %param.30) | copy-start | bytes 49156
  135.3 498.0 %reduce-scatter.4.cloned.1.call-start = ((), (), s32[]{:S(2)}) async-start(), calls=%async_computation.6 | async-start | bytes 10485760
  376.8 3.0 copy-start.4
  499.6 24.0 %slice-start = ((s8[7340032]{0:T(1024)(128)(4,1)}), s8[3145728]{0:T(1024)(128)(4,1)S(1)}, s32[]{:S(2)}) async-start(s8[7340032]{0:T(1024)(128)(4,1)} %bitcast.80), calls=%async_computation.7 | async-start | bytes 6291456
  511.0 12.7 %copy-start.2 = (bf16[32,32,4096]{2,1,0:T(8,128)(2,1)S(1)}, bf16[32,32,4096]{2,1,0:T(8,128)(2,1)}, u32[]{:S(2)}) copy-start(bf16[32,32,4096]{2,1,0:T(8,128)(2,1)} %copy.118) | copy-start | bytes 25165828
  511.0 12.7 %slice-start.1 = ((s8[7340032]{0:T(1024)(128)(4,1)}), s8[4194304]{0:T(1024)(128)(4,1)S(1)}, s32[]{:S(2)}) async-start(s8[7340032]{0:T(1024)(128)(4,1)} %bitcast.80), calls=%async_computation.8 | async-start | bytes 8388608
  511.0 21.9 %slice-start.2 = ((s8[7340032]{0:T(1024)(128)(4,1)}), s8[4194304]{0:T(1024)(128)(4,1)S(1)}, s32[]{:S(2)}) async-start(s8[7340032]{0:T(1024)(128)(4,1)} %bitcast.82), calls=%async_computation.9 | async-start | bytes 8388608
  523.7 9.2 %slice-start.3 = ((s8[7340032]{0:T(1024)(128)(4,1)}), s8[3145728]{0:T(1024)(128)(4,1)S(1)}, s32[]{:S(2)}) async-start(s8[7340032]{0:T(1024)(128)(4,1)} %bitcast.82), calls=%async_computation.10 | async-start | bytes 6291456
  555.5 86.8 %copy-start.11 = (f32[128,2]{0,1:T(2,128)S(1)}, f32[128,2]{0,1:T(2,128)}, u32[]{:S(2)}) copy-start(f32[128,2]{0,1:T(2,128)} %param.35) | copy-start | bytes 3076
  633.2 36.3 %all-to-all-start.1 = ((bf16[8,32,4096]{2,0,1:T(8,128)(2,1)}), bf16[8,32,4096]{2,0,1:T(8,128)(2,1)}, u32[]{:S(2)}, u32[]{:S(2)}) async-start(bf16[8,32,4096]{2,0,1:T(8,128)(2,1)} %bitcast.76), calls=%async_computation.1 | async-start | bytes 4194304 | tf_op jit(solution)/shard_map/all_to_all | solution.py:160
  673.5 8.0 %copy-start.1 = (bf16[128,128]{1,0:T(8,128)(2,1)S(1)}, bf16[128,128]{1,0:T(8,128)(2,1)}, u32[]{:S(2)}) copy-start(bf16[128,128]{1,0:T(8,128)(2,1)} %param.21) | copy-start | bytes 98308
Sparse Core Ops, SparseCore 0:
  11.0 56.9 all-gather.2
  70.2 59.1 all-gather.4
  135.4 241.3 all-reduce.1
  555.6 77.6 reduce-scatter.3
where the time goes:
time: 696 us; the launch traced here: 688 us
  waiting for transfers between devices  439 us (63%)
  blocking collectives  114 us (16%)
  local copies, waits for them, and re-layouts  52.4 us (8%)
  matrix products  43.4 us (6%)
  other arithmetic  17.9 us (3%)
  between operations  13.8 us (2%)
  starting transfers between devices  8.55 us (1%)
    psum x1, waiting for transfers between devices, local(): lax.psum(partial_value.astype(jnp.bfloat16), 'exp').astype(jnp.float32)  240 us
    all_to_all x1, blocking collectives, local(): lax.all_to_all(outgoing, 'ctx', split_axis=1, concat_axis=1, tiled=True)  105 us
    unnamed x5, waiting for transfers between devices  78.5 us
    all_gather x1, waiting for transfers between devices, entering(): gathered = lax.all_gather(packed.astype(jnp.bfloat16), axis)  55.4 us
    all_gather x1, waiting for transfers between devices, local(): lax.all_gather(out_proj, 'ctx', axis=1, tiled=True)  37.1 us
    all_to_all x1, waiting for transfers between devices, local(): lax.all_to_all(summed, 'ctx', split_axis=1, concat_axis=1, tiled=True)  27.1 us
  transfers between devices with their start and end apart: 5, of which 5 were waited for; matrix products, arithmetic and copies ran while one was open for 3% of the time, Pallas kernels for 0%

commit v1 on v0

--- a/solution.py
+++ b/solution.py
@@ -115,7 +115,9 @@
     normed_mix = (gated_out * scaling[:, None] * norm_gain[None, :]).astype(jnp.bfloat16)
     partial_value = jnp.dot(
         normed_mix,
-        lax.all_gather(out_proj, "ctx", axis=1, tiled=True),
+        jnp.concatenate(
+            lax.all_to_all(jnp.stack([out_proj] * lax.axis_size("ctx")), "ctx", 0, 0), axis=1
+        ),
         preferred_element_type=jnp.float32,
     )
     gate_rows = w_gate[0]

time: 696 us -> 777 us (1.12)
  waiting for transfers between devices: 439 us -> 502 us
  starting transfers between devices: 8.55 us -> 18.6 us
    all_gather x1, waiting for transfers between devices: 55.4 us -> 114 us  [entering(): gathered = lax.all_gather(packed.astype(jnp.bfloat16), axis)]
    psum x1, waiting for transfers between devices: 240 us -> 283 us  [local(): lax.psum(partial_value.astype(jnp.bfloat16), 'exp').astype(jnp.float32)]
    all_gather x1 -> x0, waiting for transfers between devices: 37.1 us -> none  [local(): lax.all_gather(out_proj, 'ctx', axis=1, tiled=True)]
    all_to_all x0 -> x1, starting transfers between devices: none -> 9.79 us  [local(): lax.all_to_all(jnp.stack([out_proj] * lax.axis_size('ctx')), 'ctx', 0, 0)]
    unnamed x5 -> x4, waiting for transfers between devices: 78.5 us -> 77.8 us
  transfers between devices with their start and end apart: 5 -> 5, of which waited for: 5 -> 4; matrix products, arithmetic and copies ran while one was open for 3% -> 3% of each run, Pallas kernels for 0% -> 0%
where the time goes in v1:
time: 777 us; the launch traced here: 768 us
  waiting for transfers between devices  502 us (65%)
  blocking collectives  113 us (15%)
  local copies, waits for them, and re-layouts  57.7 us (7%)
  matrix products  44.3 us (6%)
  starting transfers between devices  18.6 us (2%)
  other arithmetic  17.9 us (2%)
  between operations  14 us (2%)
    psum x1, waiting for transfers between devices, local(): lax.psum(partial_value.astype(jnp.bfloat16), 'exp').astype(jnp.float32)  283 us
    all_gather x1, waiting for transfers between devices, entering(): gathered = lax.all_gather(packed.astype(jnp.bfloat16), axis)  114 us
    all_to_all x1, blocking collectives, local(): lax.all_to_all(outgoing, 'ctx', split_axis=1, concat_axis=1, tiled=True)  105 us
    unnamed x4, waiting for transfers between devices  77.8 us
    all_to_all x1, waiting for transfers between devices, local(): lax.all_to_all(summed, 'ctx', split_axis=1, concat_axis=1, tiled=True)  27.1 us
  transfers between devices with their start and end apart: 5, of which 4 were waited for; matrix products, arithmetic and copies ran while one was open for 3% of the time, Pallas kernels for 0%

profile of v1, /device:TPU:1, one launch (start us, length us, event | category | flops | bytes accessed | tf_op | source)
XLA Modules:
  0.0 767.9 jit_solution(12291094136630959188)
XLA Ops:
  12.1 4.3 stack.2
  16.4 9.8 %all-to-all-start = ((bf16[32,1024,128]{1,2,0:T(8,128)(2,1)}), bf16[32,1024,128]{1,2,0:T(8,128)(2,1)}, u32[]{:S(2)}, u32[]{:S(2)}) async-start(bf16[32,1024,128]{1,2,0:T(8,128)(2,1)} %stack.2), calls=%async_computation | async-start | bytes 16777216 | tf_op jit(solution)/shard_map/all_to_all | solution.py:119
  26.4 114.2 %all-gather.2.cloned.1.call-done = bf16[32,16,65,128]{3,1,2,0:T(8,128)(2,1)} async-done(((bf16[1,16,65,128]{3,1,2,0:T(8,128)(2,1)}), bf16[32,16,65,128]{3,1,2,0:T(8,128)(2,1)}) %all-gather.2.cloned.1.call-update) | async-done | bytes 8519696 | tf_op jit(solution)/shard_map/all_gather | solution.py:17
  140.5 2.5 broadcast_in_dim.28
  143.0 8.0 %while.12 = (s32[]{:T(128)}, f32[16]{0:T(128)S(1)}, f32[16,64,128]{0,2,1:T(8,128)}, s32[]{:T(128)}, bf16[32,16,65,128]{3,1,2,0:T(8,128)(2,1)}, /*index=5*/s32[]{:T(128)}, s32[]{:T(128)}, s32[]{:T(128)}) while((s32[]{:T(128)}, f32[16]{0:T(128)S(1)}, f32[16,64,128]{0,2,1:T(8,128)}, s32[]{:T(128)}, bf16[32,16,65,128]{3,1,2,0:T(8,128)(2,1)}, ...), condition=%wide.region_2.3_spmd, body=%wide.region_1.2_spmd.sunk | while | flops 395285 | bytes 3437051 | solution.py:24
  144.0 1.4 copy.139
  146.0 5.0 slice_add_fusion.2
  151.0 2.9 copy.118
  154.4 1.4 fusion.9
  156.3 8.4 %psum.14 = f32[128]{0:T(128)S(1)} all-reduce(f32[128]{0:T(128)S(1)} %multiply_reduce_fusion.2), channel_id=1, replica_groups=mesh['ctx'=32,'exp'=4] {'exp'}, use_global_device_ids=true, to_apply=%region_4.5 | all-reduce | flops 128 | bytes 1024 | tf_op jit(solution)/shard_map/psum | solution.py:113
  164.8 7.4 convolution_convert_fusion.2
  173.5 282.8 %all-reduce.2.cloned.1.call-done = bf16[128,4096]{1,0:T(8,128)(2,1)} async-done(((bf16[128,4096]{1,0:T(8,128)(2,1)}), bf16[128,4096]{1,0:T(8,128)(2,1)}) %all-reduce.2.cloned.1.call-update) | async-done | bytes 1048592 | tf_op jit(solution)/shard_map/psum | solution.py:130
  456.4 3.0 convert_add_fusion
  459.8 3.4 broadcast_in_dim.30
  463.3 2.7 reshape.173
  466.0 1.4 convolution_convert_fusion.1
  467.4 2.3 copy.124
  469.7 4.3 broadcast_in_dim.31
  473.9 104.9 %all_to_all.15 = bf16[32,32,4096]{2,0,1:T(8,128)(2,1)} all-to-all(bf16[32,32,4096]{2,0,1:T(8,128)(2,1)} %bitcast.73), channel_id=1, replica_groups=mesh['ctx'=32,'exp'=4] {'ctx'}, dimensions={1} | all-to-all | bytes 16777216 | tf_op jit(solution)/shard_map/all_to_all | solution.py:143
  578.9 11.3 %copy.125 = bf16[32,32,4096]{2,1,0:T(8,128)(2,1)} copy(bf16[32,32,4096]{2,0,1:T(8,128)(2,1)} %all_to_all.15) | data formatting | bytes 16777216 | tf_op jit(solution)/shard_map/all_to_all | solution.py:143
  590.2 12.7 %fusion.2 = f32[1024,896]{1,0:T(8,128)S(1)} fusion(bf16[1024,4096]{1,0:T(8,128)(2,1)} %bitcast.75, bf16[1,4096,896]{2,1,0:T(8,128)(2,1)} %param.32), kind=kOutput, calls=%fused_computation.8 | convolution fusion | flops 7516192768 | bytes 19398656 | tf_op jit(solution)/shard_map/dot_general | solution.py:146
  603.0 9.2 %multiply_convert_fusion = bf16[1024,896]{1,0:T(8,128)(2,1)S(1)} fusion(f32[1024,896]{1,0:T(8,128)S(1)} %fusion.2, bf16[1024,4096]{1,0:T(8,128)(2,1)S(1)} %bitcast.76, bf16[1,4096,896]{2,1,0:T(8,128)(2,1)S(1)} %bitcast.84), kind=kOutput, calls=%fused_computation.14 | convolution fusion | flops 7521697792 | bytes 21233664 | tf_op jit(solution)/shard_map/dot_general | solution.py:145
  612.2 11.3 %convolution_convert_fusion = bf16[1024,4096]{1,0:T(8,128)(2,1)} fusion(bf16[1024,896]{1,0:T(8,128)(2,1)S(1)} %multiply_convert_fusion, bf16[1,896,4096]{2,1,0:T(8,128)(2,1)S(1)} %bitcast.86), kind=kOutput, calls=%fused_computation.6 | convolution fusion | flops 7520387072 | bytes 17563648 | tf_op jit(solution)/shard_map/dot_general | solution.py:150
  623.5 11.3 %copy.137 = bf16[4,8,32,4096]{3,1,2,0:T(8,128)(2,1)} copy(bf16[4,8,32,4096]{3,2,1,0:T(8,128)(2,1)} %bitcast.77) | data formatting | bytes 16777216
  634.8 77.8 %reduce-scatter.4.cloned.1.call-done = bf16[8,131072]{1,0:T(8,128)(2,1)} async-done(((bf16[32,131072]{1,0:T(8,128)(2,1)}), bf16[8,131072]{1,0:T(8,128)(2,1)}) %reduce-scatter.4.cloned.1.call-update) | async-done | bytes 2097168
  712.6 8.2 %all-to-all-start.2 = ((bf16[8,32,4096]{2,0,1:T(8,128)(2,1)}), bf16[8,32,4096]{2,0,1:T(8,128)(2,1)}, u32[]{:S(2)}, u32[]{:S(2)}) async-start(bf16[8,32,4096]{2,0,1:T(8,128)(2,1)} %bitcast.79), calls=%async_computation.2 | async-start | bytes 4194304 | tf_op jit(solution)/shard_map/all_to_all | solution.py:162
  721.8 27.1 %all-to-all-done.2 = bf16[8,32,4096]{2,0,1:T(8,128)(2,1)} async-done(((bf16[8,32,4096]{2,0,1:T(8,128)(2,1)}), bf16[8,32,4096]{2,0,1:T(8,128)(2,1)}, u32[]{:S(2)}, u32[]{:S(2)}) %all-to-all-start.2) | async-done | bytes 2097184 | tf_op jit(solution)/shard_map/all_to_all | solution.py:162
  748.9 2.7 copy.127
  752.9 1.3 reshape.188
  754.2 2.7 reduce_sum.60
  757.6 1.4 multiply_reduce_fusion.1
  759.0 1.8 add_convert_fusion
  (88 shorter events, 12.7 us)
Async XLA Ops:
  6.5 3.1 copy-start
  6.5 134.0 %all-gather.2.cloned.1.call-start = ((), (), s32[]{:S(2)}) async-start(), calls=%async_computation.4 | async-start | bytes 8785920 | tf_op jit(solution)/shard_map/all_gather | solution.py:17
  16.4 9.9 %copy-start.7 = (bf16[128,128]{1,0:T(8,128)(2,1)S(1)}, bf16[128,128]{1,0:T(8,128)(2,1)}, u32[]{:S(2)}) copy-start(bf16[128,128]{1,0:T(8,128)(2,1)} %param.22) | copy-start | bytes 98308
  16.4 148.4 %all-to-all-start = ((bf16[32,1024,128]{1,2,0:T(8,128)(2,1)}), bf16[32,1024,128]{1,2,0:T(8,128)(2,1)}, u32[]{:S(2)}, u32[]{:S(2)}) async-start(bf16[32,1024,128]{1,2,0:T(8,128)(2,1)} %stack.2), calls=%async_computation | async-start | bytes 16777216 | tf_op jit(solution)/shard_map/all_to_all | solution.py:119
  26.2 430.2 %all-reduce.2.cloned.1.call-start = ((), (), s32[]{:S(2)}) async-start(), calls=%async_computation.5 | async-start | bytes 2097152 | tf_op jit(solution)/shard_map/psum | solution.py:130
  151.0 3.0 copy-start.5
  151.0 3.4 copy-start.9
  151.0 3.5 copy-start.13
  151.0 5.1 copy-start.6
  153.9 10.8 %copy-start.12 = (f32[1024]{0:T(1024)S(1)}, f32[1024]{0:T(1024)}, u32[]{:S(2)}) copy-start(f32[1024]{0:T(1024)} %param.27) | copy-start | bytes 12292
  164.8 8.1 %copy-start.10 = (s32[128,2]{0,1:T(2,128)S(1)}, s32[128,2]{0,1:T(2,128)}, u32[]{:S(2)}) copy-start(s32[128,2]{0,1:T(2,128)} %param.34) | copy-start | bytes 3076
  164.8 291.6 %copy-start.3 = (bf16[128,4096]{1,0:T(8,128)(2,1)S(1)}, bf16[128,4096]{1,0:T(8,128)(2,1)}, u32[]{:S(2)}) copy-start(bf16[128,4096]{1,0:T(8,128)(2,1)} %param.29) | copy-start | bytes 3145732
  172.2 287.2 %copy-start.8 = (f32[4096]{0:T(1024)S(1)}, f32[4096]{0:T(1024)}, u32[]{:S(2)}) copy-start(f32[4096]{0:T(1024)} %param.30) | copy-start | bytes 49156
  172.3 540.3 %reduce-scatter.4.cloned.1.call-start = ((), (), s32[]{:S(2)}) async-start(), calls=%async_computation.6 | async-start | bytes 10485760
  456.4 3.0 copy-start.4
  578.9 24.0 %slice-start = ((s8[7340032]{0:T(1024)(128)(4,1)}), s8[3145728]{0:T(1024)(128)(4,1)S(1)}, s32[]{:S(2)}) async-start(s8[7340032]{0:T(1024)(128)(4,1)} %bitcast.83), calls=%async_computation.7 | async-start | bytes 6291456
  590.2 12.7 %copy-start.2 = (bf16[32,32,4096]{2,1,0:T(8,128)(2,1)S(1)}, bf16[32,32,4096]{2,1,0:T(8,128)(2,1)}, u32[]{:S(2)}) copy-start(bf16[32,32,4096]{2,1,0:T(8,128)(2,1)} %copy.125) | copy-start | bytes 25165828
  590.2 12.7 %slice-start.1 = ((s8[7340032]{0:T(1024)(128)(4,1)}), s8[4194304]{0:T(1024)(128)(4,1)S(1)}, s32[]{:S(2)}) async-start(s8[7340032]{0:T(1024)(128)(4,1)} %bitcast.83), calls=%async_computation.8 | async-start | bytes 8388608
  590.2 21.9 %slice-start.2 = ((s8[7340032]{0:T(1024)(128)(4,1)}), s8[4194304]{0:T(1024)(128)(4,1)S(1)}, s32[]{:S(2)}) async-start(s8[7340032]{0:T(1024)(128)(4,1)} %bitcast.85), calls=%async_computation.9 | async-start | bytes 8388608
  603.0 9.2 %slice-start.3 = ((s8[7340032]{0:T(1024)(128)(4,1)}), s8[3145728]{0:T(1024)(128)(4,1)S(1)}, s32[]{:S(2)}) async-start(s8[7340032]{0:T(1024)(128)(4,1)} %bitcast.85), calls=%async_computation.10 | async-start | bytes 6291456
  634.8 86.8 %copy-start.11 = (f32[128,2]{0,1:T(2,128)S(1)}, f32[128,2]{0,1:T(2,128)}, u32[]{:S(2)}) copy-start(f32[128,2]{0,1:T(2,128)} %param.35) | copy-start | bytes 3076
  712.6 36.3 %all-to-all-start.2 = ((bf16[8,32,4096]{2,0,1:T(8,128)(2,1)}), bf16[8,32,4096]{2,0,1:T(8,128)(2,1)}, u32[]{:S(2)}, u32[]{:S(2)}) async-start(bf16[8,32,4096]{2,0,1:T(8,128)(2,1)} %bitcast.79), calls=%async_computation.2 | async-start | bytes 4194304 | tf_op jit(solution)/shard_map/all_to_all | solution.py:162
  752.9 8.0 %copy-start.1 = (bf16[128,128]{1,0:T(8,128)(2,1)S(1)}, bf16[128,128]{1,0:T(8,128)(2,1)}, u32[]{:S(2)}) copy-start(bf16[128,128]{1,0:T(8,128)(2,1)} %param.21) | copy-start | bytes 98308
Sparse Core Ops, SparseCore 0:
  11.1 129.4 all-gather.1
  172.4 283.9 all-reduce.1
  634.9 77.6 reduce-scatter.3
